TPU v7x, 32 devices: a whole 2x2x4 slice. The times are simulated.
32 devices in a mesh: frames: 8 (over z, x), heads: 4 (over y, core).
Axes of the slice: x: 2, y: 2, z: 4, core: 2. Of those that a mesh axis runs over, the one named last changes fastest.
Arguments:
- queries: bfloat16 [1024, 4096], P('frames', 'heads'), may hold values from -9 to 9
- keys: bfloat16 [1024, 512], P(('frames', 'heads')), may hold values from -4.5 to 4.5
- values: bfloat16 [1024, 512], P(('frames', 'heads')), may hold values from -6 to 6
- block_mask: int32 [8, 8], replicated, may hold values from 0 to 1, as said below
- lengths: int32 [8], replicated, may hold values from 64 to 128, as said below
Outputs:
- attended: bfloat16 [1024, 4096], P('frames', 'heads')
Inputs may be any that keep to these rules, and one draw needn't show every extreme that they name: block_mask[i, i] = 1 and block_mask[i, j] = 0 for j > i. `lengths`: some frame group is full in every draw.
All inputs are finite; a program needn't handle non-finite values.
Results may differ from a plain program's by a relative error of at most 0.0055.
Values may be sent and summed in bfloat16 or wider, within the bound.
A program may use at most 64 MiB of HBM per device.

v0:
```python
import math
import jax
import jax.numpy as jnp
from jax import lax
from jax.sharding import PartitionSpec as P

HEAD_DIM = 128
masked_score = -1e30


def attend(query_sets, keys_mine, values_mine, block_mask, lengths, group_tokens):
    kv_local = keys_mine.shape[1] // HEAD_DIM
    q_local = query_sets[0][0].shape[1] // HEAD_DIM
    per_kv = q_local // kv_local
    scale = HEAD_DIM ** (-0.5)
    group_count = block_mask.shape[0]
    group_ids = jnp.arange(group_count, dtype=jnp.int32)
    prepared = []
    initial = []
    for rows, owner in query_sets:
        count = rows.shape[0]
        prepared.append(
            (
                rows.reshape(count, kv_local, per_kv, HEAD_DIM),
                lax.dynamic_slice_in_dim(block_mask, owner, 1, 0)[0],
            )
        )
        initial.append(
            (
                jnp.full((kv_local, per_kv, count), masked_score, jnp.float32),
                jnp.zeros((kv_local, per_kv, count), jnp.float32),
                jnp.zeros((count, kv_local, per_kv, HEAD_DIM), jnp.float32),
            )
        )
    key_piece = lax.all_gather(keys_mine, "frames", axis=0, tiled=True)
    value_piece = lax.all_gather(values_mine, "frames", axis=0, tiled=True)
    fold_rows = key_piece.shape[0]
    width = math.gcd(fold_rows, 512)
    blocks = fold_rows // width
    key_blocks = key_piece.reshape(blocks, width, kv_local, HEAD_DIM)
    value_blocks = value_piece.reshape(blocks, width, kv_local, HEAD_DIM)

    def one_block(state, inputs):
        key_block, value_block, number = inputs
        positions = number * width + jnp.arange(width, dtype=jnp.int32)
        key_group = positions // group_tokens
        within = positions % group_tokens
        onehot = (key_group[:, None] == group_ids[None, :]).astype(jnp.int32)
        live_len = jnp.sum(onehot * lengths[None, :], axis=1)
        updated = []
        for (query_rows, mask_row), (running_max, running_total, running_acc) in zip(
            prepared, state
        ):
            allowed = jnp.sum(onehot * mask_row[None, :], axis=1)
            valid = (allowed > 0) & (within < live_len)

            def update(current):
                old_max, old_total, old_acc = current
                scores = (
                    jnp.einsum(
                        "tkgd,skd->kgts", query_rows, key_block, preferred_element_type=jnp.float32
                    )
                    * scale
                )
                scores = jnp.where(valid[None, None, None, :], scores, masked_score)
                new_max = jnp.maximum(old_max, jnp.max(scores, axis=-1))
                probs = jnp.exp(scores - new_max[..., None])
                factor = jnp.exp(old_max - new_max)
                new_total = old_total * factor + jnp.sum(probs, axis=-1)
                added = jnp.einsum(
                    "kgts,skd->tkgd",
                    probs.astype(jnp.bfloat16),
                    value_block,
                    preferred_element_type=jnp.float32,
                )
                new_acc = old_acc * jnp.transpose(factor, (2, 0, 1))[..., None] + added
                return (new_max, new_total, new_acc)

            updated.append(
                lax.cond(
                    jnp.any(valid),
                    update,
                    lambda current: current,
                    (running_max, running_total, running_acc),
                )
            )
        return (tuple(updated), None)

    numbers = jnp.arange(blocks, dtype=jnp.int32)
    final, unused = lax.scan(one_block, tuple(initial), (key_blocks, value_blocks, numbers))
    results = []
    for (rows, owner), (running_max, running_total, running_acc) in zip(query_sets, final):
        output = running_acc / jnp.transpose(running_total, (2, 0, 1))[..., None]
        results.append(output.astype(jnp.bfloat16).reshape(rows.shape[0], q_local * HEAD_DIM))
    return results


def local(queries, keys, values, block_mask, lengths):
    keys_mine, values_mine = (
        lax.all_to_all(keys, "heads", split_axis=1, concat_axis=0, tiled=True),
        lax.all_to_all(values, "heads", split_axis=1, concat_axis=0, tiled=True),
    )
    group_tokens = queries.shape[0]
    frame_index = lax.axis_index("frames")
    outputs = attend(
        [(queries, frame_index)], keys_mine, values_mine, block_mask, lengths, group_tokens
    )
    return outputs[0]


def solution(mesh):
    return jax.shard_map(
        local,
        mesh=mesh,
        in_specs=(
            P("frames", "heads"),
            P(("frames", "heads"), None),
            P(("frames", "heads"), None),
            P(),
            P(),
        ),
        out_specs=P("frames", "heads"),
        check_vma=False,
    )
```

profile of v0, /device:TPU:30, one launch (start us, length us, event | category | flops | bytes accessed | tf_op | source)
XLA Modules:
  0.0 84.3 jit_solution(984634713009666700)
XLA Ops:
  0.0 0.8 copy-done
  0.8 0.6 copy_bitcast_fusion
  1.4 3.7 %all-to-all-start.1 = ((bf16[32,4,128]{2,0,1:T(8,128)(2,1)}), bf16[32,4,128]{2,0,1:T(8,128)(2,1)S(1)}, u32[]{:S(2)}, u32[]{:S(2)}) async-start(bf16[32,4,128]{2,0,1:T(8,128)(2,1)} %copy_bitcast_fusion), calls=%async_computation.1 | async-start | bytes 65536 | tf_op jit(solution)/shard_map/all_to_all | solution.py:101
  5.1 1.4 %copy_bitcast_fusion.1 = bf16[32,4,128]{2,0,1:T(8,128)(2,1)} fusion(bf16[32,512]{1,0:T(8,128)(2,1)} %param.10), kind=kLoop, calls=%fused_computation.47 | loop fusion | bytes 65536 | tf_op jit(solution)/shard_map/all_to_all | solution.py:100
  6.5 0.7 constant_dynamic-slice_fusion
  7.2 1.1 %copy.37 = bf16[128,1024]{0,1:T(8,128)(2,1)S(1)} copy(bf16[128,1024]{1,0:T(8,128)(2,1)} %param.9) | data formatting | bytes 524288 | tf_op args[0]
  8.3 0.2 copy.39
  8.5 3.8 %all-to-all-start = ((bf16[32,4,128]{2,0,1:T(8,128)(2,1)}), bf16[32,4,128]{2,0,1:T(8,128)(2,1)S(1)}, u32[]{:S(2)}, u32[]{:S(2)}) async-start(bf16[32,4,128]{2,0,1:T(8,128)(2,1)} %copy_bitcast_fusion.1), calls=%async_computation | async-start | bytes 65536 | tf_op jit(solution)/shard_map/all_to_all | solution.py:100
  12.3 30.8 %all_gather.7 = bf16[1024,128]{1,0:T(8,128)(2,1)S(1)} all-gather(bf16[128,128]{1,0:T(8,128)(2,1)S(1)} %bitcast.97), channel_id=1, replica_groups=mesh['frames'=8,'heads'=4] {'frames'}, dimensions={0}, use_global_device_ids=true | all-gather | bytes 294912 | tf_op jit(solution)/shard_map/all_gather | solution.py:36
  43.3 30.7 %all_gather.6 = bf16[1024,128]{1,0:T(8,128)(2,1)S(1)} all-gather(bf16[128,128]{1,0:T(8,128)(2,1)S(1)} %bitcast.98), channel_id=1, replica_groups=mesh['frames'=8,'heads'=4] {'frames'}, dimensions={0}, use_global_device_ids=true | all-gather | bytes 294912 | tf_op jit(solution)/shard_map/all_gather | solution.py:35
  74.1 9.3 %while.17 = (s32[]{:T(128)}, f32[1,8,128]{2,1,0:T(8,128)S(1)}, f32[1,8,128]{2,1,0:T(8,128)S(1)}, f32[128,1,8,128]{0,3,2,1:T(8,128)S(1)}, s32[2]{0:T(128)S(1)}, /...) while((s32[]{:T(128)}, f32[1,8,128]{2,1,0:T(8,128)S(1)}, ...), condition=%wide.region_8.9_spmd.clone, body=%wide.region_0.8_spmd.clone.sunk | while | flops 274503680 | bytes 7944539 | solution.py:90
  74.1 0.6 dynamic_slice.43
  75.4 0.7 fusion.39
  76.9 1.9 %conditional.3 = ((f32[1,8,128]{2,1,0:T(8,128)S(1)}, f32[1,8,128]{2,1,0:T(8,128)S(1)}, f32[128,1,8,128]{0,3,2,1:T(8,128)S(1)})) conditional(s32[]{:T(128)} %convert_element_type.23, (f32[1,8,128]{2,1,0:T(8,128)S(1)}, f32[1,8,128]{2,1,0:T(8,128)S(1)}, f32[128,1,8,128]{0,3,2,1:T(8,128)S(1)}) %tuple.59, (pred[512]{0:T(512)(128)(4,1)S(1)}, ...), branch_computations={%region_4.4_spmd, %region_5.7_spmd} | conditional | flops 274467840 | bytes 7931432 | solution.py:80
  76.9 0.5 bitcast_reduce_fusion
  77.4 0.8 fusion.5
  78.2 0.5 fusion.4
  78.7 0.6 dynamic_slice.43
  80.1 0.7 fusion.39
  81.5 1.9 %conditional.3 = ((f32[1,8,128]{2,1,0:T(8,128)S(1)}, f32[1,8,128]{2,1,0:T(8,128)S(1)}, f32[128,1,8,128]{0,3,2,1:T(8,128)S(1)})) conditional(s32[]{:T(128)} %convert_element_type.23, (f32[1,8,128]{2,1,0:T(8,128)S(1)}, f32[1,8,128]{2,1,0:T(8,128)S(1)}, f32[128,1,8,128]{0,3,2,1:T(8,128)S(1)}) %tuple.59, (pred[512]{0:T(512)(128)(4,1)S(1)}, ...), branch_computations={%region_4.4_spmd, %region_5.7_spmd} | conditional | flops 274467840 | bytes 7931432 | solution.py:80
  81.5 0.5 bitcast_reduce_fusion
  82.0 0.8 fusion.5
  82.9 0.5 fusion.4
  83.5 0.9 %copy.43 = bf16[128,1024]{1,0:T(8,128)(2,1)} copy(bf16[128,1024]{0,1:T(8,128)(2,1)S(1)} %bitcast.93) | data formatting | bytes 524288 | tf_op jit(solution)/shard_map/reshape | solution.py:94
  (21 shorter events, 0.5 us)
Async XLA Ops:
  0.0 0.8 copy-start
  0.8 73.3 %copy-start.1 = (s32[8]{0:T(128)S(1)}, s32[8]{0:T(128)}, u32[]{:S(2)}) copy-start(s32[8]{0:T(128)} %param.13) | copy-start | bytes 100
  1.4 7.1 %all-to-all-start.1 = ((bf16[32,4,128]{2,0,1:T(8,128)(2,1)}), bf16[32,4,128]{2,0,1:T(8,128)(2,1)S(1)}, u32[]{:S(2)}, u32[]{:S(2)}) async-start(bf16[32,4,128]{2,0,1:T(8,128)(2,1)} %copy_bitcast_fusion), calls=%async_computation.1 | async-start | bytes 65536 | tf_op jit(solution)/shard_map/all_to_all | solution.py:101
  8.5 34.8 %all-to-all-start = ((bf16[32,4,128]{2,0,1:T(8,128)(2,1)}), bf16[32,4,128]{2,0,1:T(8,128)(2,1)S(1)}, u32[]{:S(2)}, u32[]{:S(2)}) async-start(bf16[32,4,128]{2,0,1:T(8,128)(2,1)} %copy_bitcast_fusion.1), calls=%async_computation | async-start | bytes 65536 | tf_op jit(solution)/shard_map/all_to_all | solution.py:100
where the time goes:
time: 84.8 us; the launch traced here: 84.3 us
  blocking collectives  61.6 us (73%)
  starting transfers between devices  7.53 us (9%)
  local copies, waits for them, and re-layouts  6.95 us (8%)
  loops' own time  2.87 us (3%)
  other arithmetic  2.72 us (3%)
  matrix products  2.59 us (3%)
    all_gather x1, blocking collectives, attend(): value_piece = lax.all_gather(values_mine, 'frames', axis=0, tiled=True)  30.8 us
    all_gather x1, blocking collectives, attend(): key_piece = lax.all_gather(keys_mine, 'frames', axis=0, tiled=True)  30.7 us
    all_to_all x1, starting transfers between devices, local(): lax.all_to_all(keys, 'heads', split_axis=1, concat_axis=0, tiled=True)  3.79 us
    all_to_all x1, starting transfers between devices, local(): lax.all_to_all(values, 'heads', split_axis=1, concat_axis=0, tiled=True)  3.74 us
    another operation x1, loops' own time, attend(): lax.scan(one_block, tuple(initial), (key_blocks, value_blocks, numbers))  2.76 us
    unnamed x7, local copies, waits for them, and re-layouts  2.2 us
  transfers between devices with their start and end apart: 2, of which 0 were waited for; matrix products, arithmetic and copies ran while one was open for 4% of the time, Pallas kernels for 0%

commit v1 on v0

--- a/solution.py
+++ b/solution.py
@@ -6,6 +6,13 @@
 
 HEAD_DIM = 128
 masked_score = -1e30
+
+
+def trade_parts(x, axis, split, join):
+    size = lax.axis_size(axis)
+    blocks = jnp.stack(jnp.split(x, size, axis=split), axis=0)
+    blocks = lax.all_to_all(blocks, axis, split_axis=0, concat_axis=0)
+    return jnp.concatenate(blocks, axis=join)
 
 
 def attend(query_sets, keys_mine, values_mine, block_mask, lengths, group_tokens):
@@ -97,7 +104,7 @@
 
 def local(queries, keys, values, block_mask, lengths):
     keys_mine, values_mine = (
-        lax.all_to_all(keys, "heads", split_axis=1, concat_axis=0, tiled=True),
+        trade_parts(keys, "heads", 1, 0),
         lax.all_to_all(values, "heads", split_axis=1, concat_axis=0, tiled=True),
     )
     group_tokens = queries.shape[0]

time: 84.8 us -> 84.3 us (level)
  local copies, waits for them, and re-layouts: 6.95 us -> 5.59 us
    all_to_all x1 -> x0, local copies, waits for them, and re-layouts: 1.38 us -> none  [local(): lax.all_to_all(keys, 'heads', split_axis=1, concat_axis=0, tiled=True)]
  transfers between devices with their start and end apart: 2 -> 2, of which waited for: 0 -> 0; matrix products, arithmetic and copies ran while one was open for 4% -> 3% of each run, Pallas kernels for 0% -> 0%
where the time goes in v1:
time: 84.3 us; the launch traced here: 83.9 us
  blocking collectives  61.6 us (73%)
  starting transfers between devices  8.28 us (10%)
  local copies, waits for them, and re-layouts  5.59 us (7%)
  other arithmetic  3.17 us (4%)
  loops' own time  2.61 us (3%)
  matrix products  2.59 us (3%)
    all_gather x1, blocking collectives, attend(): key_piece = lax.all_gather(keys_mine, 'frames', axis=0, tiled=True)  30.8 us
    all_gather x1, blocking collectives, attend(): value_piece = lax.all_gather(values_mine, 'frames', axis=0, tiled=True)  30.7 us
    all_to_all x1, starting transfers between devices, local(): lax.all_to_all(values, 'heads', split_axis=1, concat_axis=0, tiled=True)  4.54 us
    all_to_all x1, starting transfers between devices, trade_parts(): blocks = lax.all_to_all(blocks, axis, split_axis=0, concat_axis=0)  3.74 us
    another operation x1, loops' own time, attend(): lax.scan(one_block, tuple(initial), (key_blocks, value_blocks, numbers))  2.5 us
  transfers between devices with their start and end apart: 2, of which 0 were waited for; matrix products, arithmetic and copies ran while one was open for 3% of the time, Pallas kernels for 0%

profile of v1, /device:TPU:30, one launch (start us, length us, event | category | flops | bytes accessed | tf_op | source)
XLA Modules:
  0.0 83.9 jit_solution(12553481389251819885)
XLA Ops:
  0.0 0.8 slice_bitcast_fusion.3
  0.8 0.6 pad_maximum_fusion
  1.4 3.7 %all-to-all-start = ((bf16[4,32,128]{2,1,0:T(8,128)(2,1)}), bf16[4,32,128]{2,1,0:T(8,128)(2,1)S(1)}, u32[]{:S(2)}, u32[]{:S(2)}) async-start(bf16[4,32,128]{2,1,0:T(8,128)(2,1)} %pad_maximum_fusion), calls=%async_computation | async-start | bytes 65536 | tf_op jit(solution)/shard_map/all_to_all | solution.py:14
  5.1 0.6 copy_bitcast_fusion
  5.8 0.7 constant_dynamic-slice_fusion
  6.4 1.1 %copy.26 = bf16[128,1024]{0,1:T(8,128)(2,1)S(1)} copy(bf16[128,1024]{1,0:T(8,128)(2,1)} %param.9) | data formatting | bytes 524288 | tf_op args[0]
  7.6 0.2 copy.28
  7.8 4.5 %all-to-all-start.1 = ((bf16[32,4,128]{2,0,1:T(8,128)(2,1)}), bf16[32,4,128]{2,0,1:T(8,128)(2,1)S(1)}, u32[]{:S(2)}, u32[]{:S(2)}) async-start(bf16[32,4,128]{2,0,1:T(8,128)(2,1)} %copy_bitcast_fusion), calls=%async_computation.1 | async-start | bytes 65536 | tf_op jit(solution)/shard_map/all_to_all | solution.py:108
  12.3 30.8 %all_gather.6 = bf16[1024,128]{1,0:T(8,128)(2,1)S(1)} all-gather(bf16[128,128]{1,0:T(8,128)(2,1)S(1)} %bitcast.98), channel_id=1, replica_groups=mesh['frames'=8,'heads'=4] {'frames'}, dimensions={0}, use_global_device_ids=true | all-gather | bytes 294912 | tf_op jit(solution)/shard_map/all_gather | solution.py:42
  43.1 30.7 %all_gather.7 = bf16[1024,128]{1,0:T(8,128)(2,1)S(1)} all-gather(bf16[128,128]{1,0:T(8,128)(2,1)S(1)} %bitcast.99), channel_id=1, replica_groups=mesh['frames'=8,'heads'=4] {'frames'}, dimensions={0}, use_global_device_ids=true | all-gather | bytes 294912 | tf_op jit(solution)/shard_map/all_gather | solution.py:43
  74.1 8.9 %while.17 = (s32[]{:T(128)}, f32[1,8,128]{2,1,0:T(8,128)S(1)}, f32[1,8,128]{2,1,0:T(8,128)S(1)}, f32[128,1,8,128]{0,3,2,1:T(8,128)S(1)}, s32[2]{0:T(128)S(1)}, /...) while((s32[]{:T(128)}, f32[1,8,128]{2,1,0:T(8,128)S(1)}, ...), condition=%wide.region_8.9_spmd.clone, body=%wide.region_0.8_spmd.clone.sunk | while | flops 274503680 | bytes 7944539 | solution.py:97
  74.1 0.6 dynamic_slice.43
  75.5 0.6 fusion.38
  76.7 1.9 %conditional.3 = ((f32[1,8,128]{2,1,0:T(8,128)S(1)}, f32[1,8,128]{2,1,0:T(8,128)S(1)}, f32[128,1,8,128]{0,3,2,1:T(8,128)S(1)})) conditional(s32[]{:T(128)} %convert_element_type.23, (f32[1,8,128]{2,1,0:T(8,128)S(1)}, f32[1,8,128]{2,1,0:T(8,128)S(1)}, f32[128,1,8,128]{0,3,2,1:T(8,128)S(1)}) %tuple.61, (pred[512]{0:T(512)(128)(4,1)S(1)}, ...), branch_computations={%region_4.4_spmd, %region_5.7_spmd} | conditional | flops 274467840 | bytes 7931432 | solution.py:87
  76.7 0.5 bitcast_reduce_fusion
  77.2 0.8 %fusion.5 = f32[128,1,8,128]{0,3,2,1:T(8,128)S(1)} fusion(f32[512,128,8]{1,0,2:T(8,128)S(1)} %get-tuple-element.322, f32[8,128]{1,0:T(8,128)S(1)} %bitcast.92, pred[512]{0:T(512)(128)(4,1)S(1)} %get-tuple-element.204, f32[128,1,8,128]{0,3,2,1:T(8,128)S(1)} %get-tuple-element.209, f32[128,8]{0,1:T(8,128)S(1)} %get-tuple-element.317, ...), kind=kOutput, calls=%fused_computation.8 | convolution fusion | flops 136577024 | bytes 3285508 | tf_op jit(solution)/shard_map/while/body/eval_jaxpr/cond/branch_1_fun/kgts,skd->tkgd/dot_general | solution.py:77
  78.0 0.5 fusion.4
  78.6 0.6 dynamic_slice.43
  79.9 0.6 fusion.38
  81.1 1.9 %conditional.3 = ((f32[1,8,128]{2,1,0:T(8,128)S(1)}, f32[1,8,128]{2,1,0:T(8,128)S(1)}, f32[128,1,8,128]{0,3,2,1:T(8,128)S(1)})) conditional(s32[]{:T(128)} %convert_element_type.23, (f32[1,8,128]{2,1,0:T(8,128)S(1)}, f32[1,8,128]{2,1,0:T(8,128)S(1)}, f32[128,1,8,128]{0,3,2,1:T(8,128)S(1)}) %tuple.61, (pred[512]{0:T(512)(128)(4,1)S(1)}, ...), branch_computations={%region_4.4_spmd, %region_5.7_spmd} | conditional | flops 274467840 | bytes 7931432 | solution.py:87
  81.1 0.5 bitcast_reduce_fusion
  81.6 0.8 %fusion.5 = f32[128,1,8,128]{0,3,2,1:T(8,128)S(1)} fusion(f32[512,128,8]{1,0,2:T(8,128)S(1)} %get-tuple-element.322, f32[8,128]{1,0:T(8,128)S(1)} %bitcast.92, pred[512]{0:T(512)(128)(4,1)S(1)} %get-tuple-element.204, f32[128,1,8,128]{0,3,2,1:T(8,128)S(1)} %get-tuple-element.209, f32[128,8]{0,1:T(8,128)S(1)} %get-tuple-element.317, ...), kind=kOutput, calls=%fused_computation.8 | convolution fusion | flops 136577024 | bytes 3285508 | tf_op jit(solution)/shard_map/while/body/eval_jaxpr/cond/branch_1_fun/kgts,skd->tkgd/dot_general | solution.py:77
  82.4 0.5 fusion.4
  83.0 0.9 %copy.32 = bf16[128,1024]{1,0:T(8,128)(2,1)} copy(bf16[128,1024]{0,1:T(8,128)(2,1)S(1)} %bitcast.94) | data formatting | bytes 524288 | tf_op jit(solution)/shard_map/reshape | solution.py:101
  (22 shorter events, 0.5 us)
Async XLA Ops:
  0.0 5.1 %copy-start = (bf16[32,512]{1,0:T(8,128)(2,1)S(1)}, bf16[32,512]{1,0:T(8,128)(2,1)}, u32[]{:S(2)}) copy-start(bf16[32,512]{1,0:T(8,128)(2,1)} %param.11) | copy-start | bytes 98308
  0.0 74.1 %copy-start.1 = (s32[8]{0:T(128)S(1)}, s32[8]{0:T(128)}, u32[]{:S(2)}) copy-start(s32[8]{0:T(128)} %param.13) | copy-start | bytes 100
  1.4 6.4 %all-to-all-start = ((bf16[4,32,128]{2,1,0:T(8,128)(2,1)}), bf16[4,32,128]{2,1,0:T(8,128)(2,1)S(1)}, u32[]{:S(2)}, u32[]{:S(2)}) async-start(bf16[4,32,128]{2,1,0:T(8,128)(2,1)} %pad_maximum_fusion), calls=%async_computation | async-start | bytes 65536 | tf_op jit(solution)/shard_map/all_to_all | solution.py:14
  7.8 35.4 %all-to-all-start.1 = ((bf16[32,4,128]{2,0,1:T(8,128)(2,1)}), bf16[32,4,128]{2,0,1:T(8,128)(2,1)S(1)}, u32[]{:S(2)}, u32[]{:S(2)}) async-start(bf16[32,4,128]{2,0,1:T(8,128)(2,1)} %copy_bitcast_fusion), calls=%async_computation.1 | async-start | bytes 65536 | tf_op jit(solution)/shard_map/all_to_all | solution.py:108
